TPU v7x, 32 devices: a whole 2x2x4 slice. The times are simulated.
32 devices in a mesh: dp: 16 (over z, y, x), mp: 2 (over core).
Axes of the slice: x: 2, y: 2, z: 4, core: 2. Of those that a mesh axis runs over, the one named last changes fastest.
Arguments:
- residual: bfloat16 [256, 4608], P(None, 'dp'), may hold values from -60 to 60
- norm_gain: float32 [4608], P('dp'), may hold values from 0.25 to 1.75
- query_weight: bfloat16 [4608, 2048], P('dp', 'mp'), may hold values from -2 to 2
- key_weight: bfloat16 [4608, 1024], P('dp', 'mp'), may hold values from -2 to 2
- value_weight: bfloat16 [4608, 1024], P('dp', 'mp'), may hold values from -0.09375 to 0.09375
- out_weight: bfloat16 [2048, 4608], P('mp', 'dp'), may hold values from -1 to 1
- post_gain: float32 [4608], P('dp'), may hold values from 0.25 to 1.75
- encoder_weight: bfloat16 [4608, 8192], P(None, ('dp', 'mp')), may hold values from -0.09375 to 0.09375
- encoder_bias: float32 [8192], P(('dp', 'mp')), may hold values from -3 to 3
- decoder_weight: bfloat16 [8192, 4608], P(('dp', 'mp')), may hold values from -0.125 to 0.125
- decoder_bias: float32 [4608], replicated, may hold values from -3 to 3
Outputs:
- encoder_grad: bfloat16 [4608, 8192], P(None, ('dp', 'mp'))
- encoder_bias_grad: float32 [8192], P(('dp', 'mp'))
- decoder_grad: bfloat16 [8192, 4608], P(('dp', 'mp'))
All inputs are finite; a program needn't handle non-finite values.
Results may differ from a plain program's by a relative error of at most 0.015.
Values may be sent and summed in bfloat16 or wider, within the bound.
No kernel may reach another device: no remote copies, remote signals or barrier semaphores. Data moves between devices by JAX's collectives and lax.ppermute only.
A program may use at most 128 MiB of HBM per device.

v0:
```python
import jax
import jax.numpy as jnp
from jax import lax
from jax.sharding import PartitionSpec as P

HEAD_DIM = 128
epsilon = 1e-06
softcap = 50.0
query_scale = 1.0 / 12.0
rope_base = 10000.0
smoothing = 0.1
penalty = 1.0
loss_weight = 0.0625


def rotate(matrix, positions):
    half_dim = matrix.shape[-1] // 2
    frequency = rope_base ** (-2.0 * jnp.arange(half_dim, dtype=jnp.float32) / matrix.shape[-1])
    angles = positions.astype(jnp.float32)[:, None] * frequency[None, :]
    cosine = jnp.cos(angles)[:, None, :]
    sine_part = jnp.sin(angles)[:, None, :]
    front_half = matrix[..., :half_dim]
    back_half = matrix[..., half_dim:]
    return jnp.concatenate(
        [front_half * cosine - back_half * sine_part, back_half * cosine + front_half * sine_part],
        axis=-1,
    )


def project(summed, square_sum, positions, model_width, query_width, key_width, head_dim):
    inverse = lax.rsqrt(square_sum / model_width + epsilon)
    scaled = summed * inverse[:, None]
    row_count = scaled.shape[0]
    queries = rotate(scaled[:, :query_width].reshape(row_count, -1, head_dim), positions).astype(
        jnp.bfloat16
    )
    keys = rotate(
        scaled[:, query_width : query_width + key_width].reshape(row_count, -1, head_dim), positions
    ).astype(jnp.bfloat16)
    values = (
        scaled[:, query_width + key_width :].reshape(row_count, -1, head_dim).astype(jnp.bfloat16)
    )
    return (queries, keys, values)


def partial_attention(queries, keys, values, query_positions, key_positions):
    row_count, query_heads, head_dim = queries.shape
    key_heads = keys.shape[1]
    grouped = queries.reshape(row_count, key_heads, query_heads // key_heads, head_dim)
    scores = (
        jnp.einsum("rkgd,skd->kgrs", grouped, keys, preferred_element_type=jnp.float32)
        * query_scale
    )
    capped = softcap * jnp.tanh(scores / softcap)
    allowed = query_positions[:, None] >= key_positions[None, :]
    weights = jnp.where(allowed, jnp.exp(capped), 0.0)
    denominator = jnp.sum(weights, axis=3)
    numerator = jnp.einsum(
        "kgrs,skd->rkgd", weights.astype(jnp.bfloat16), values, preferred_element_type=jnp.float32
    )
    return (
        numerator.reshape(row_count, query_heads, head_dim),
        jnp.transpose(denominator, (2, 0, 1)).reshape(row_count, query_heads),
    )


def on_device(
    residual,
    norm_gain,
    query_weight,
    key_weight,
    value_weight,
    out_weight,
    post_gain,
    encoder_weight,
    encoder_bias,
    decoder_weight,
    decoder_bias,
):
    token_count = residual.shape[0]
    model_width = decoder_weight.shape[1]
    head_dim = HEAD_DIM
    query_width = query_weight.shape[1]
    key_width = key_weight.shape[1]
    residual_float = residual.astype(jnp.float32)
    scaled = (residual_float * norm_gain).astype(jnp.bfloat16)
    stacked = jnp.concatenate([query_weight, key_weight, value_weight], axis=1)
    projected_part = jnp.dot(scaled, stacked, preferred_element_type=jnp.float32)
    partial_squares = jnp.sum(residual_float * residual_float, axis=1)
    summed, square_sum = lax.psum((projected_part, partial_squares), "dp")
    positions = jnp.arange(token_count)
    queries, keys, values = project(
        summed, square_sum, positions, model_width, query_width, key_width, head_dim
    )
    numerator, denominator = partial_attention(queries, keys, values, positions, positions)
    attended = (
        (numerator / denominator[:, :, None]).astype(jnp.bfloat16).reshape(token_count, query_width)
    )
    heads_part = jnp.dot(attended, out_weight, preferred_element_type=jnp.float32)
    head_out = lax.psum(heads_part, "mp")
    out_squares = lax.psum(jnp.sum(head_out * head_out, axis=1), "dp")
    normed = head_out * lax.rsqrt(out_squares / model_width + epsilon)[:, None] * post_gain
    hidden_columns = (residual_float + normed).astype(jnp.bfloat16)
    portion = lax.all_gather(hidden_columns, "dp", axis=1, tiled=True)
    preact_sum = jnp.dot(portion, encoder_weight, preferred_element_type=jnp.float32)
    preact_sum, hidden = (preact_sum, portion)
    preact = preact_sum + encoder_bias
    active = smoothing * jax.nn.softplus(preact / smoothing)
    active_low = active.astype(jnp.bfloat16)
    gate_slope = jax.nn.sigmoid(preact / smoothing)
    decoder_norms = jnp.sqrt(
        jnp.sum(jnp.square(decoder_weight.astype(jnp.float32)), axis=1) + epsilon
    )
    activity = jnp.sum(active, axis=0)
    rebuilt_part = jnp.dot(active_low, decoder_weight, preferred_element_type=jnp.float32)
    rebuilt = lax.psum(rebuilt_part, ("dp", "mp"))
    error_low = (rebuilt + decoder_bias - hidden.astype(jnp.float32)).astype(jnp.bfloat16)
    feedback = lax.dot_general(
        error_low, decoder_weight, (((1,), (1,)), ((), ())), preferred_element_type=jnp.float32
    )
    outer_sum = lax.dot_general(
        active_low, error_low, (((0,), (0,)), ((), ())), preferred_element_type=jnp.float32
    )
    grad_active = loss_weight * (2.0 * feedback + penalty * decoder_norms)
    grad_preact = grad_active * gate_slope
    encoder_grad = lax.dot_general(
        hidden,
        grad_preact.astype(jnp.bfloat16),
        (((0,), (0,)), ((), ())),
        preferred_element_type=jnp.float32,
    ).astype(jnp.bfloat16)
    encoder_bias_grad = jnp.sum(grad_preact, axis=0)
    decoder_grad = (
        loss_weight
        * (
            2.0 * outer_sum
            + penalty * (activity / decoder_norms)[:, None] * decoder_weight.astype(jnp.float32)
        )
    ).astype(jnp.bfloat16)
    return (encoder_grad, encoder_bias_grad, decoder_grad)


def solution(mesh):
    placed = (
        P(None, "dp"),
        P("dp"),
        P("dp", "mp"),
        P("dp", "mp"),
        P("dp", "mp"),
        P("mp", "dp"),
        P("dp"),
        P(None, ("dp", "mp")),
        P(("dp", "mp")),
        P(("dp", "mp"), None),
        P(),
    )
    return jax.shard_map(
        on_device,
        mesh=mesh,
        in_specs=placed,
        out_specs=(P(None, ("dp", "mp")), P(("dp", "mp")), P(("dp", "mp"), None)),
        check_vma=False,
    )
```

profile of v0, /device:TPU:0, one launch (start us, length us, event | category | flops | bytes accessed | tf_op | source)
XLA Modules:
  0.0 448.3 jit_solution(4388165543059884381)
XLA Ops:
  7.2 0.0 copy-start
  7.2 0.0 all-reduce.4.cloned.1.call-start
  7.2 3.6 fusion.4
  10.9 0.0 all-reduce.4.cloned.1.call-update
  10.9 0.0 all-reduce.6.cloned.1.call-start
  10.9 0.1 fusion.21
  11.0 44.4 %psum.36 = f32[256]{0:T(256)S(1)} all-reduce(f32[256]{0:T(256)S(1)} %fusion.21), channel_id=1, replica_groups=mesh['dp'=16,'mp'=2] {'dp'}, use_global_device_ids=true, to_apply=%region_2.0 | all-reduce | flops 256 | bytes 2048 | tf_op jit(solution)/shard_map/psum | solution.py:90
  55.4 0.7 iota_compare_fusion
  56.1 1.3 multiply_cosine_fusion
  57.4 85.9 %all-reduce.4.cloned.1.call-done = f32[256,2048]{1,0:T(8,128)} async-done(((f32[256,2048]{1,0:T(8,128)}), f32[256,2048]{1,0:T(8,128)}) %all-reduce.4.cloned.1.call-update) | async-done | bytes 2097168 | tf_op jit(solution)/shard_map/psum | solution.py:90
  143.2 1.8 broadcast_multiply_fusion
  145.1 1.0 slice_bitcast_fusion
  146.1 0.8 slice.42
  146.9 0.2 reshape.99
  147.1 1.1 fusion.36
  148.2 0.1 copy-done.4
  148.3 0.2 copy.28
  148.5 0.5 subtract_convert_fusion.1
  149.0 0.9 copy.16
  149.9 0.9 copy.17
  150.8 1.8 copy.25
  152.6 1.1 subtract_convert_fusion.2
  153.7 3.3 fusion.37
  157.0 1.6 fusion.15
  158.6 0.0 copy-start.12
  158.6 0.0 copy-start.13
  158.6 0.1 fusion.14
  158.7 1.0 fusion.39
  159.8 0.0 all-reduce.6.cloned.1.call-update
  159.8 0.0 all-gather.2.cloned.1.call-start
  159.8 17.8 %all-reduce.6.cloned.1.call-done = f32[256,288]{0,1:T(8,128)} async-done(((f32[256,288]{0,1:T(8,128)}), f32[256,288]{0,1:T(8,128)}) %all-reduce.6.cloned.1.call-update) | async-done | bytes 294928 | tf_op jit(solution)/shard_map/psum | solution.py:100
  177.6 1.0 multiply_reduce_fusion
  178.6 42.0 %psum.38 = f32[256]{0:T(256)S(1)} all-reduce(f32[256]{0:T(256)S(1)} %multiply_reduce_fusion), channel_id=1, replica_groups=mesh['dp'=16,'mp'=2] {'dp'}, use_global_device_ids=true, to_apply=%region_6.7 | all-reduce | flops 256 | bytes 2048 | tf_op jit(solution)/shard_map/psum | solution.py:101
  220.6 1.7 fusion.22
  222.3 0.0 all-gather.2.cloned.1.call-update
  222.4 0.2 all-reduce.8.cloned.1.call-start
  222.6 58.1 %all-gather.2.cloned.1.call-done = bf16[256,4608]{0,1:T(8,128)(2,1)} async-done(((bf16[256,288]{0,1:T(8,128)(2,1)}), bf16[256,4608]{0,1:T(8,128)(2,1)}) %all-gather.2.cloned.1.call-update) | async-done | bytes 2359312 | tf_op jit(solution)/shard_map/all_gather | solution.py:104
  280.7 2.8 fusion.29
  283.5 3.3 fusion.34
  286.8 0.0 all-reduce.8.cloned.1.call-update
  286.8 0.0 copy-start.11
  286.8 2.2 fusion.3
  289.0 141.6 %all-reduce.8.cloned.1.call-done = f32[256,4608]{0,1:T(8,128)} async-done(((f32[256,4608]{0,1:T(8,128)}), f32[256,4608]{0,1:T(8,128)}) %all-reduce.8.cloned.1.call-update) | async-done | bytes 4718608 | tf_op jit(solution)/shard_map/psum | solution.py:116
  430.6 4.2 subtract_convert_fusion
  434.9 3.1 fusion.2
  438.0 1.4 fusion.38
  439.4 0.3 copy-done.1
  439.6 2.2 convolution_convert_fusion
  (29 shorter events, 0.1 us)
Async XLA Ops:
  7.2 273.5 %copy-start = (bf16[4608,256]{1,0:T(8,128)(2,1)S(1)}, bf16[4608,256]{1,0:T(8,128)(2,1)}, u32[]{:S(2)}) copy-start(bf16[4608,256]{1,0:T(8,128)(2,1)} %param.18) | copy-start | bytes 7077892
  7.2 3.8 copy-start.6
  7.2 136.0 %all-reduce.4.cloned.1.call-start = ((), (), s32[]{:S(2)}) async-start(), calls=%async_computation | async-start | bytes 4194304 | tf_op jit(solution)/shard_map/psum | solution.py:90
  10.9 166.7 %all-reduce.6.cloned.1.call-start = ((), (), s32[]{:S(2)}) async-start(), calls=%async_computation.1 | async-start | bytes 589824 | tf_op jit(solution)/shard_map/psum | solution.py:100
  147.1 1.2 copy-start.4
  147.1 1.4 copy-start.7
  147.1 1.4 copy-start.8
  148.5 4.1 copy-start.5
  153.7 3.3 copy-start.9
  157.0 1.7 copy-start.10
  158.6 62.0 %copy-start.12 = (f32[288]{0:T(512)S(1)}, f32[288]{0:T(512)}, u32[]{:S(2)}) copy-start(f32[288]{0:T(512)} %param.17) | copy-start | bytes 3460
  158.6 122.1 %copy-start.13 = (f32[256]{0:T(256)S(1)}, f32[256]{0:T(256)}, u32[]{:S(2)}) copy-start(f32[256]{0:T(256)} %param.19) | copy-start | bytes 3076
  159.8 120.9 %all-gather.2.cloned.1.call-start = ((), (), s32[]{:S(2)}) async-start(), calls=%async_computation.2 | async-start | bytes 2506752 | tf_op jit(solution)/shard_map/all_gather | solution.py:104
  222.4 208.3 %all-reduce.8.cloned.1.call-start = ((), (), s32[]{:S(2)}) async-start(), calls=%async_computation.3 | async-start | bytes 9437184 | tf_op jit(solution)/shard_map/psum | solution.py:116
  280.7 2.8 copy-start.2
  286.8 143.8 %copy-start.11 = (f32[4608]{0:T(1024)S(1)}, f32[4608]{0:T(1024)}, u32[]{:S(2)}) copy-start(f32[4608]{0:T(1024)} %param.21) | copy-start | bytes 55300
  430.6 4.3 copy-start.3
  438.0 1.7 copy-start.1
Sparse Core Ops, SparseCore 0:
  14.1 129.1 all-reduce.3
  159.9 17.6 all-reduce.5
  222.5 58.1 all-gather.1
  287.1 143.4 all-reduce.7
where the time goes:
time: 449 us; the launch traced here: 448 us
  waiting for transfers between devices  303 us (67%)
  blocking collectives  86.3 us (19%)
  matrix products  22.3 us (5%)
  other arithmetic  14.7 us (3%)
  between operations  14 us (3%)
  local copies, waits for them, and re-layouts  7.29 us (2%)
    psum x1, waiting for transfers between devices, on_device(): rebuilt = lax.psum(rebuilt_part, ('dp', 'mp'))  142 us
    psum x1, waiting for transfers between devices, on_device(): summed, square_sum = lax.psum((projected_part, partial_squares), 'dp')  85.9 us
    all_gather x1, waiting for transfers between devices, on_device(): portion = lax.all_gather(hidden_columns, 'dp', axis=1, tiled=True)  58.1 us
    psum x1, blocking collectives, on_device(): summed, square_sum = lax.psum((projected_part, partial_squares), 'dp')  44.4 us
    psum x1, blocking collectives, on_device(): out_squares = lax.psum(jnp.sum(head_out * head_out, axis=1), 'dp')  42 us
    psum x1, waiting for transfers between devices, on_device(): head_out = lax.psum(heads_part, 'mp')  17.8 us
  transfers between devices with their start and end apart: 4, of which 4 were waited for; matrix products, arithmetic and copies ran while one was open for 1% of the time, Pallas kernels for 0%

commit v1 on v0

--- a/solution.py
+++ b/solution.py
@@ -101,7 +101,27 @@
     out_squares = lax.psum(jnp.sum(head_out * head_out, axis=1), "dp")
     normed = head_out * lax.rsqrt(out_squares / model_width + epsilon)[:, None] * post_gain
     hidden_columns = (residual_float + normed).astype(jnp.bfloat16)
-    portion = lax.all_gather(hidden_columns, "dp", axis=1, tiled=True)
+    plain = lax.psum(1, "dp")
+    q_next = lax.axis_index("dp")
+    k_now, met_up, high = (plain, q_next, hidden_columns.shape[1])
+    found = tuple(
+        (dev_j * k_now if b == 1 else dev_j for b, dev_j in enumerate(hidden_columns.shape))
+    )
+    r_now = jnp.zeros(found, hidden_columns.dtype)
+    portion = lax.dynamic_update_slice_in_dim(r_now, hidden_columns, met_up * high, axis=1)
+    outer = tmp = hidden_columns
+    for d in range(1, k_now // 2 + 1):
+        taken_in = tuple(((b, (b + 1) % k_now) for b in range(k_now)))
+        outer = lax.ppermute(outer, "dp", perm=taken_in)
+        portion = lax.dynamic_update_slice_in_dim(
+            portion, outer, (met_up - d) % k_now * high, axis=1
+        )
+        if 2 * d < k_now:
+            current_block = tuple(((b, (b - 1) % k_now) for b in range(k_now)))
+            tmp = lax.ppermute(tmp, "dp", current_block)
+            portion = lax.dynamic_update_slice_in_dim(
+                portion, tmp, (met_up + d) % k_now * high, axis=1
+            )
     preact_sum = jnp.dot(portion, encoder_weight, preferred_element_type=jnp.float32)
     preact_sum, hidden = (preact_sum, portion)
     preact = preact_sum + encoder_bias

time: 449 us -> 519 us (1.16)
  local copies, waits for them, and re-layouts: 7.29 us -> 69.1 us
  starting transfers between devices: 0.34 us -> 39.7 us
  waiting for transfers between devices: 303 us -> 271 us
    all_gather x1 -> x0, waiting for transfers between devices: 58.1 us -> none  [on_device(): portion = lax.all_gather(hidden_columns, 'dp', axis=1, tiled=True)]
    dynamic_update_slice x0 -> x16, local copies, waits for them, and re-layouts: none -> 55.8 us  [the longest x8 27.6 us: on_device(): lax.dynamic_update_slice_in_dim(portion, outer, (met_up - d) % k_now * hi...]
    ppermute x0 -> x15, starting transfers between devices: none -> 39.6 us  [the longest x7 39.5 us: on_device(): tmp = lax.ppermute(tmp, 'dp', current_block)]
    ppermute x0 -> x15, waiting for transfers between devices: none -> 23.7 us  [the longest x8 23.6 us: on_device(): outer = lax.ppermute(outer, 'dp', perm=taken_in)]
  transfers between devices with their start and end apart: 4 -> 18, of which waited for: 4 -> 10; matrix products, arithmetic and copies ran while one was open for 1% -> 12% of each run, Pallas kernels for 0% -> 0%
where the time goes in v1:
time: 519 us; the launch traced here: 516 us
  waiting for transfers between devices  271 us (52%)
  blocking collectives  86.5 us (17%)
  local copies, waits for them, and re-layouts  69.1 us (13%)
  starting transfers between devices  39.7 us (8%)
  matrix products  21.7 us (4%)
  between operations  14.5 us (3%)
  other arithmetic  13.5 us (3%)
    psum x1, waiting for transfers between devices, on_device(): rebuilt = lax.psum(rebuilt_part, ('dp', 'mp'))  144 us
    psum x1, waiting for transfers between devices, on_device(): summed, square_sum = lax.psum((projected_part, partial_squares), 'dp')  85.9 us
    psum x1, blocking collectives, on_device(): summed, square_sum = lax.psum((projected_part, partial_squares), 'dp')  44.4 us
    psum x1, blocking collectives, on_device(): out_squares = lax.psum(jnp.sum(head_out * head_out, axis=1), 'dp')  42.1 us
    ppermute x7, starting transfers between devices, on_device(): tmp = lax.ppermute(tmp, 'dp', current_block)  39.5 us
    dynamic_update_slice x8, local copies, waits for them, and re-layouts, on_device(): lax.dynamic_update_slice_in_dim(portion, outer, (met_up - d) % k_now * hi...  27.6 us
    dynamic_update_slice x7, local copies, waits for them, and re-layouts, on_device(): lax.dynamic_update_slice_in_dim(portion, tmp, (met_up + d) % k_now * high...  25 us
    ppermute x8, waiting for transfers between devices, on_device(): outer = lax.ppermute(outer, 'dp', perm=taken_in)  23.6 us
  transfers between devices with their start and end apart: 18, of which 10 were waited for; matrix products, arithmetic and copies ran while one was open for 12% of the time, Pallas kernels for 0%

profile of v1, /device:TPU:0, one launch (start us, length us, event | category | flops | bytes accessed | tf_op | source)
XLA Modules:
  0.0 516.5 jit_solution(10015215001062204689)
XLA Ops:
  7.2 3.6 fusion.4
  11.0 44.4 %psum.36 = f32[256]{0:T(256)S(1)} all-reduce(f32[256]{0:T(256)S(1)} %fusion.21), channel_id=1, replica_groups=mesh['dp'=16,'mp'=2] {'dp'}, use_global_device_ids=true, to_apply=%region_2.0 | all-reduce | flops 256 | bytes 2048 | tf_op jit(solution)/shard_map/psum | solution.py:90
  57.3 85.9 %all-reduce.4.cloned.1.call-done = f32[256,2048]{1,0:T(8,128)} async-done(((f32[256,2048]{1,0:T(8,128)}), f32[256,2048]{1,0:T(8,128)}) %all-reduce.4.cloned.1.call-update) | async-done | bytes 2097168 | tf_op jit(solution)/shard_map/psum | solution.py:90
  143.2 1.8 broadcast_multiply_fusion
  150.8 1.8 copy.39
  153.7 3.3 fusion.37
  157.0 1.6 fusion.15
  159.8 17.8 %all-reduce.6.cloned.1.call-done = f32[256,288]{0,1:T(8,128)} async-done(((f32[256,288]{0,1:T(8,128)}), f32[256,288]{0,1:T(8,128)}) %all-reduce.6.cloned.1.call-update) | async-done | bytes 294928 | tf_op jit(solution)/shard_map/psum | solution.py:100
  178.6 42.1 %psum.38 = f32[256]{0:T(256)S(1)} all-reduce(f32[256]{0:T(256)S(1)} %multiply_reduce_fusion), channel_id=1, replica_groups=mesh['dp'=16,'mp'=2] {'dp'}, use_global_device_ids=true, to_apply=%region_6.7 | all-reduce | flops 256 | bytes 2048 | tf_op jit(solution)/shard_map/psum | solution.py:101
  221.8 5.6 %collective-permute-start.1 = (bf16[256,288]{0,1:T(8,128)(2,1)S(1)}, bf16[256,288]{0,1:T(8,128)(2,1)S(1)}, u32[]{:S(2)}, u32[]{:S(2)}) collective-permute-start(bf16[256,288]{0,1:T(8,128)(2,1)S(1)} %fusion.22), channel_id=1, source_target_pairs={{0,30},{2,0},{4,2},{6,4},{8,6},{10,8},{12,10},{14,12},{16,14},{18,... | collective-permute-start | bytes 442376 | tf_op jit(solution)/shard_map/ppermute | solution.py:121
  227.5 4.4 collective-permute-done
  231.9 5.6 %collective-permute-start.3 = (bf16[256,288]{0,1:T(8,128)(2,1)S(1)}, bf16[256,288]{0,1:T(8,128)(2,1)S(1)}, u32[]{:S(2)}, u32[]{:S(2)}) collective-permute-start(bf16[256,288]{0,1:T(8,128)(2,1)S(1)} %collective-permute-done.1), channel_id=1, source_target_pairs={{0,30},{2,0},{4,2},{6,4},{8,6},{10,8},{12,10},{14,12},{16,14},{18,... | collective-permute-start | bytes 442376 | tf_op jit(solution)/shard_map/ppermute | solution.py:121
  237.5 3.6 collective-permute-done.2
  241.1 5.6 %collective-permute-start.5 = (bf16[256,288]{0,1:T(8,128)(2,1)S(1)}, bf16[256,288]{0,1:T(8,128)(2,1)S(1)}, u32[]{:S(2)}, u32[]{:S(2)}) collective-permute-start(bf16[256,288]{0,1:T(8,128)(2,1)S(1)} %collective-permute-done.3), channel_id=1, source_target_pairs={{0,30},{2,0},{4,2},{6,4},{8,6},{10,8},{12,10},{14,12},{16,14},{18,... | collective-permute-start | bytes 442376 | tf_op jit(solution)/shard_map/ppermute | solution.py:121
  246.7 3.2 collective-permute-done.4
  250.0 5.6 %collective-permute-start.7 = (bf16[256,288]{0,1:T(8,128)(2,1)S(1)}, bf16[256,288]{0,1:T(8,128)(2,1)S(1)}, u32[]{:S(2)}, u32[]{:S(2)}) collective-permute-start(bf16[256,288]{0,1:T(8,128)(2,1)S(1)} %collective-permute-done.5), channel_id=1, source_target_pairs={{0,30},{2,0},{4,2},{6,4},{8,6},{10,8},{12,10},{14,12},{16,14},{18,... | collective-permute-start | bytes 442376 | tf_op jit(solution)/shard_map/ppermute | solution.py:121
  255.6 3.1 collective-permute-done.6
  258.7 5.7 %collective-permute-start.9 = (bf16[256,288]{0,1:T(8,128)(2,1)S(1)}, bf16[256,288]{0,1:T(8,128)(2,1)S(1)}, u32[]{:S(2)}, u32[]{:S(2)}) collective-permute-start(bf16[256,288]{0,1:T(8,128)(2,1)S(1)} %collective-permute-done.7), channel_id=1, source_target_pairs={{0,30},{2,0},{4,2},{6,4},{8,6},{10,8},{12,10},{14,12},{16,14},{18,... | collective-permute-start | bytes 442376 | tf_op jit(solution)/shard_map/ppermute | solution.py:121
  264.4 3.1 collective-permute-done.8
  267.5 5.6 %collective-permute-start.11 = (bf16[256,288]{0,1:T(8,128)(2,1)S(1)}, bf16[256,288]{0,1:T(8,128)(2,1)S(1)}, u32[]{:S(2)}, u32[]{:S(2)}) collective-permute-start(bf16[256,288]{0,1:T(8,128)(2,1)S(1)} %collective-permute-done.9), channel_id=1, source_target_pairs={{0,30},{2,0},{4,2},{6,4},{8,6},{10,8},{12,10},{14,12},{16,14},{18,... | collective-permute-start | bytes 442376 | tf_op jit(solution)/shard_map/ppermute | solution.py:121
  273.2 3.2 collective-permute-done.10
  276.3 5.7 %collective-permute-start.13 = (bf16[256,288]{0,1:T(8,128)(2,1)S(1)}, bf16[256,288]{0,1:T(8,128)(2,1)}, u32[]{:S(2)}, u32[]{:S(2)}) collective-permute-start(bf16[256,288]{0,1:T(8,128)(2,1)S(1)} %collective-permute-done.11), channel_id=1, source_target_pairs={{0,30},{2,0},{4,2},{6,4},{8,6},{10,8},{12,10},{14,12},{16,14},{18,... | collective-permute-start | bytes 442376 | tf_op jit(solution)/shard_map/ppermute | solution.py:121
  282.0 3.1 collective-permute-done.12
  285.6 1.6 broadcast_in_dim.8
  287.2 3.2 dynamic_update_slice.48
  290.6 3.0 dynamic_update_slice.49
  293.8 3.6 dynamic_update_slice.50
  297.6 3.6 dynamic_update_slice.51
  301.4 3.6 dynamic_update_slice.52
  305.2 3.6 dynamic_update_slice.53
  309.0 3.6 dynamic_update_slice.54
  312.8 3.3 dynamic_update_slice.55
  316.3 3.3 dynamic_update_slice.56
  319.8 3.6 dynamic_update_slice.57
  323.5 3.6 dynamic_update_slice.58
  327.3 3.6 dynamic_update_slice.59
  331.1 3.6 dynamic_update_slice.60
  334.8 3.6 dynamic_update_slice.61
  339.5 3.6 dynamic_update_slice.62
  344.2 3.3 dynamic_update_slice.63
  347.4 2.7 fusion.29
  350.2 3.1 fusion.34
  353.3 2.2 fusion.3
  355.5 144.0 %all-reduce.8.cloned.1.call-done = f32[256,4608]{1,0:T(8,128)} async-done(((f32[256,4608]{1,0:T(8,128)}), f32[256,4608]{1,0:T(8,128)}) %all-reduce.8.cloned.1.call-update) | async-done | bytes 4718608 | tf_op jit(solution)/shard_map/psum | solution.py:136
  499.6 3.8 subtract_convert_fusion
  503.4 2.7 fusion.2
  506.0 1.4 fusion.38
  507.7 2.2 convolution_convert_fusion
  (121 shorter events, 17.0 us)
Async XLA Ops:
  7.2 340.3 %copy-start = (bf16[4608,256]{1,0:T(8,128)(2,1)S(1)}, bf16[4608,256]{1,0:T(8,128)(2,1)}, u32[]{:S(2)}) copy-start(bf16[4608,256]{1,0:T(8,128)(2,1)} %param.18) | copy-start | bytes 7077892
  7.2 3.8 copy-start.6
  7.2 136.0 %all-reduce.4.cloned.1.call-start = ((), (), s32[]{:S(2)}) async-start(), calls=%async_computation | async-start | bytes 4194304 | tf_op jit(solution)/shard_map/psum | solution.py:90
  10.9 166.7 %all-reduce.6.cloned.1.call-start = ((), (), s32[]{:S(2)}) async-start(), calls=%async_computation.1 | async-start | bytes 589824 | tf_op jit(solution)/shard_map/psum | solution.py:100
  147.0 1.2 copy-start.4
  147.1 1.4 copy-start.7
  147.1 1.4 copy-start.8
  148.5 4.1 copy-start.5
  153.7 3.3 copy-start.9
  157.0 1.7 copy-start.10
  158.6 62.1 %copy-start.28 = (f32[288]{0:T(512)S(1)}, f32[288]{0:T(512)}, u32[]{:S(2)}) copy-start(f32[288]{0:T(512)} %param.17) | copy-start | bytes 3460
  159.8 339.8 %all-reduce.8.cloned.1.call-start = ((), (), s32[]{:S(2)}) async-start(), calls=%async_computation.2 | async-start | bytes 9437184 | tf_op jit(solution)/shard_map/psum | solution.py:136
  221.8 10.1 %collective-permute-start = (bf16[256,288]{0,1:T(8,128)(2,1)S(1)}, bf16[256,288]{0,1:T(8,128)(2,1)S(1)}, u32[]{:S(2)}, u32[]{:S(2)}) collective-permute-start(bf16[256,288]{0,1:T(8,128)(2,1)S(1)} %fusion.22), channel_id=1, source_target_pairs={{0,2},{2,4},{4,6},{6,8},{8,10},{10,12},{12,14},{14,16},{16,18},{18... | collective-permute-start | bytes 442376 | tf_op jit(solution)/shard_map/ppermute | solution.py:115
  221.8 10.1 %collective-permute-start.1 = (bf16[256,288]{0,1:T(8,128)(2,1)S(1)}, bf16[256,288]{0,1:T(8,128)(2,1)S(1)}, u32[]{:S(2)}, u32[]{:S(2)}) collective-permute-start(bf16[256,288]{0,1:T(8,128)(2,1)S(1)} %fusion.22), channel_id=1, source_target_pairs={{0,30},{2,0},{4,2},{6,4},{8,6},{10,8},{12,10},{14,12},{16,14},{18,... | collective-permute-start | bytes 442376 | tf_op jit(solution)/shard_map/ppermute | solution.py:121
  231.9 9.2 %collective-permute-start.2 = (bf16[256,288]{0,1:T(8,128)(2,1)S(1)}, bf16[256,288]{0,1:T(8,128)(2,1)S(1)}, u32[]{:S(2)}, u32[]{:S(2)}) collective-permute-start(bf16[256,288]{0,1:T(8,128)(2,1)S(1)} %collective-permute-done), channel_id=1, source_target_pairs={{0,2},{2,4},{4,6},{6,8},{8,10},{10,12},{12,14},{14,16},{16,18},{18... | collective-permute-start | bytes 442376 | tf_op jit(solution)/shard_map/ppermute | solution.py:115
  231.9 9.2 %collective-permute-start.3 = (bf16[256,288]{0,1:T(8,128)(2,1)S(1)}, bf16[256,288]{0,1:T(8,128)(2,1)S(1)}, u32[]{:S(2)}, u32[]{:S(2)}) collective-permute-start(bf16[256,288]{0,1:T(8,128)(2,1)S(1)} %collective-permute-done.1), channel_id=1, source_target_pairs={{0,30},{2,0},{4,2},{6,4},{8,6},{10,8},{12,10},{14,12},{16,14},{18,... | collective-permute-start | bytes 442376 | tf_op jit(solution)/shard_map/ppermute | solution.py:121
  241.1 8.8 %collective-permute-start.4 = (bf16[256,288]{0,1:T(8,128)(2,1)S(1)}, bf16[256,288]{0,1:T(8,128)(2,1)S(1)}, u32[]{:S(2)}, u32[]{:S(2)}) collective-permute-start(bf16[256,288]{0,1:T(8,128)(2,1)S(1)} %collective-permute-done.2), channel_id=1, source_target_pairs={{0,2},{2,4},{4,6},{6,8},{8,10},{10,12},{12,14},{14,16},{16,18},{18... | collective-permute-start | bytes 442376 | tf_op jit(solution)/shard_map/ppermute | solution.py:115
  241.1 32.1 %copy-start.11 = (bf16[256,288]{0,1:T(8,128)(2,1)}, bf16[256,288]{0,1:T(8,128)(2,1)S(1)}, u32[]{:S(2)}) copy-start(bf16[256,288]{0,1:T(8,128)(2,1)S(1)} %collective-permute-done.3) | copy-start | bytes 442372
  241.1 8.8 %collective-permute-start.5 = (bf16[256,288]{0,1:T(8,128)(2,1)S(1)}, bf16[256,288]{0,1:T(8,128)(2,1)S(1)}, u32[]{:S(2)}, u32[]{:S(2)}) collective-permute-start(bf16[256,288]{0,1:T(8,128)(2,1)S(1)} %collective-permute-done.3), channel_id=1, source_target_pairs={{0,30},{2,0},{4,2},{6,4},{8,6},{10,8},{12,10},{14,12},{16,14},{18,... | collective-permute-start | bytes 442376 | tf_op jit(solution)/shard_map/ppermute | solution.py:121
  249.9 17.6 %copy-start.13 = (bf16[256,288]{0,1:T(8,128)(2,1)}, bf16[256,288]{0,1:T(8,128)(2,1)S(1)}, u32[]{:S(2)}) copy-start(bf16[256,288]{0,1:T(8,128)(2,1)S(1)} %collective-permute-done.4) | copy-start | bytes 442372
  249.9 8.7 %collective-permute-start.6 = (bf16[256,288]{0,1:T(8,128)(2,1)S(1)}, bf16[256,288]{0,1:T(8,128)(2,1)S(1)}, u32[]{:S(2)}, u32[]{:S(2)}) collective-permute-start(bf16[256,288]{0,1:T(8,128)(2,1)S(1)} %collective-permute-done.4), channel_id=1, source_target_pairs={{0,2},{2,4},{4,6},{6,8},{8,10},{10,12},{12,14},{14,16},{16,18},{18... | collective-permute-start | bytes 442376 | tf_op jit(solution)/shard_map/ppermute | solution.py:115
  249.9 35.1 %copy-start.15 = (bf16[256,288]{0,1:T(8,128)(2,1)}, bf16[256,288]{0,1:T(8,128)(2,1)S(1)}, u32[]{:S(2)}) copy-start(bf16[256,288]{0,1:T(8,128)(2,1)S(1)} %collective-permute-done.5) | copy-start | bytes 442372
  250.0 8.7 %collective-permute-start.7 = (bf16[256,288]{0,1:T(8,128)(2,1)S(1)}, bf16[256,288]{0,1:T(8,128)(2,1)S(1)}, u32[]{:S(2)}, u32[]{:S(2)}) collective-permute-start(bf16[256,288]{0,1:T(8,128)(2,1)S(1)} %collective-permute-done.5), channel_id=1, source_target_pairs={{0,30},{2,0},{4,2},{6,4},{8,6},{10,8},{12,10},{14,12},{16,14},{18,... | collective-permute-start | bytes 442376 | tf_op jit(solution)/shard_map/ppermute | solution.py:121
  258.7 26.4 %copy-start.17 = (bf16[256,288]{0,1:T(8,128)(2,1)}, bf16[256,288]{0,1:T(8,128)(2,1)S(1)}, u32[]{:S(2)}) copy-start(bf16[256,288]{0,1:T(8,128)(2,1)S(1)} %collective-permute-done.6) | copy-start | bytes 442372
  258.7 8.8 %collective-permute-start.8 = (bf16[256,288]{0,1:T(8,128)(2,1)S(1)}, bf16[256,288]{0,1:T(8,128)(2,1)S(1)}, u32[]{:S(2)}, u32[]{:S(2)}) collective-permute-start(bf16[256,288]{0,1:T(8,128)(2,1)S(1)} %collective-permute-done.6), channel_id=1, source_target_pairs={{0,2},{2,4},{4,6},{6,8},{8,10},{10,12},{12,14},{14,16},{16,18},{18... | collective-permute-start | bytes 442376 | tf_op jit(solution)/shard_map/ppermute | solution.py:115
  258.7 26.4 %copy-start.19 = (bf16[256,288]{0,1:T(8,128)(2,1)}, bf16[256,288]{0,1:T(8,128)(2,1)S(1)}, u32[]{:S(2)}) copy-start(bf16[256,288]{0,1:T(8,128)(2,1)S(1)} %collective-permute-done.7) | copy-start | bytes 442372
  258.7 8.8 %collective-permute-start.9 = (bf16[256,288]{0,1:T(8,128)(2,1)S(1)}, bf16[256,288]{0,1:T(8,128)(2,1)S(1)}, u32[]{:S(2)}, u32[]{:S(2)}) collective-permute-start(bf16[256,288]{0,1:T(8,128)(2,1)S(1)} %collective-permute-done.7), channel_id=1, source_target_pairs={{0,30},{2,0},{4,2},{6,4},{8,6},{10,8},{12,10},{14,12},{16,14},{18,... | collective-permute-start | bytes 442376 | tf_op jit(solution)/shard_map/ppermute | solution.py:121
  267.5 17.6 %copy-start.21 = (bf16[256,288]{0,1:T(8,128)(2,1)}, bf16[256,288]{0,1:T(8,128)(2,1)S(1)}, u32[]{:S(2)}) copy-start(bf16[256,288]{0,1:T(8,128)(2,1)S(1)} %collective-permute-done.8) | copy-start | bytes 442372
  267.5 8.8 %collective-permute-start.10 = (bf16[256,288]{0,1:T(8,128)(2,1)S(1)}, bf16[256,288]{0,1:T(8,128)(2,1)S(1)}, u32[]{:S(2)}, u32[]{:S(2)}) collective-permute-start(bf16[256,288]{0,1:T(8,128)(2,1)S(1)} %collective-permute-done.8), channel_id=1, source_target_pairs={{0,2},{2,4},{4,6},{6,8},{8,10},{10,12},{12,14},{14,16},{16,18},{18... | collective-permute-start | bytes 442376 | tf_op jit(solution)/shard_map/ppermute | solution.py:115
  267.5 17.6 %copy-start.23 = (bf16[256,288]{0,1:T(8,128)(2,1)}, bf16[256,288]{0,1:T(8,128)(2,1)S(1)}, u32[]{:S(2)}) copy-start(bf16[256,288]{0,1:T(8,128)(2,1)S(1)} %collective-permute-done.9) | copy-start | bytes 442372
  267.5 8.8 %collective-permute-start.11 = (bf16[256,288]{0,1:T(8,128)(2,1)S(1)}, bf16[256,288]{0,1:T(8,128)(2,1)S(1)}, u32[]{:S(2)}, u32[]{:S(2)}) collective-permute-start(bf16[256,288]{0,1:T(8,128)(2,1)S(1)} %collective-permute-done.9), channel_id=1, source_target_pairs={{0,30},{2,0},{4,2},{6,4},{8,6},{10,8},{12,10},{14,12},{16,14},{18,... | collective-permute-start | bytes 442376 | tf_op jit(solution)/shard_map/ppermute | solution.py:121
  276.3 8.8 %copy-start.25 = (bf16[256,288]{0,1:T(8,128)(2,1)}, bf16[256,288]{0,1:T(8,128)(2,1)S(1)}, u32[]{:S(2)}) copy-start(bf16[256,288]{0,1:T(8,128)(2,1)S(1)} %collective-permute-done.10) | copy-start | bytes 442372
  276.3 8.7 %collective-permute-start.12 = (bf16[256,288]{0,1:T(8,128)(2,1)S(1)}, bf16[256,288]{0,1:T(8,128)(2,1)S(1)}, u32[]{:S(2)}, u32[]{:S(2)}) collective-permute-start(bf16[256,288]{0,1:T(8,128)(2,1)S(1)} %collective-permute-done.10), channel_id=1, source_target_pairs={{0,2},{2,4},{4,6},{6,8},{8,10},{10,12},{12,14},{14,16},{16,18},{18... | collective-permute-start | bytes 442376 | tf_op jit(solution)/shard_map/ppermute | solution.py:115
  276.3 62.1 %collective-permute-start.13 = (bf16[256,288]{0,1:T(8,128)(2,1)S(1)}, bf16[256,288]{0,1:T(8,128)(2,1)}, u32[]{:S(2)}, u32[]{:S(2)}) collective-permute-start(bf16[256,288]{0,1:T(8,128)(2,1)S(1)} %collective-permute-done.11), channel_id=1, source_target_pairs={{0,30},{2,0},{4,2},{6,4},{8,6},{10,8},{12,10},{14,12},{16,14},{18,... | collective-permute-start | bytes 442376 | tf_op jit(solution)/shard_map/ppermute | solution.py:121
  285.1 58.0 %collective-permute-start.14 = (bf16[256,288]{0,1:T(8,128)(2,1)S(1)}, bf16[256,288]{0,1:T(8,128)(2,1)}, u32[]{:S(2)}, u32[]{:S(2)}) collective-permute-start(bf16[256,288]{0,1:T(8,128)(2,1)S(1)} %collective-permute-done.12), channel_id=1, source_target_pairs={{0,2},{2,4},{4,6},{6,8},{8,10},{10,12},{12,14},{14,16},{16,18},{18... | collective-permute-start | bytes 442376 | tf_op jit(solution)/shard_map/ppermute | solution.py:115
  285.6 15.6 %copy-start.12 = (bf16[256,288]{0,1:T(8,128)(2,1)S(1)}, bf16[256,288]{0,1:T(8,128)(2,1)}, u32[]{:S(2)}) copy-start(bf16[256,288]{0,1:T(8,128)(2,1)} %copy-done.11) | copy-start | bytes 442372
  290.6 14.4 %copy-start.14 = (bf16[256,288]{0,1:T(8,128)(2,1)S(1)}, bf16[256,288]{0,1:T(8,128)(2,1)}, u32[]{:S(2)}) copy-start(bf16[256,288]{0,1:T(8,128)(2,1)} %copy-done.13) | copy-start | bytes 442372
  293.8 15.0 %copy-start.16 = (bf16[256,288]{0,1:T(8,128)(2,1)S(1)}, bf16[256,288]{0,1:T(8,128)(2,1)}, u32[]{:S(2)}) copy-start(bf16[256,288]{0,1:T(8,128)(2,1)} %copy-done.15) | copy-start | bytes 442372
  297.6 15.0 %copy-start.18 = (bf16[256,288]{0,1:T(8,128)(2,1)S(1)}, bf16[256,288]{0,1:T(8,128)(2,1)}, u32[]{:S(2)}) copy-start(bf16[256,288]{0,1:T(8,128)(2,1)} %copy-done.17) | copy-start | bytes 442372
  301.4 14.8 %copy-start.20 = (bf16[256,288]{0,1:T(8,128)(2,1)S(1)}, bf16[256,288]{0,1:T(8,128)(2,1)}, u32[]{:S(2)}) copy-start(bf16[256,288]{0,1:T(8,128)(2,1)} %copy-done.19) | copy-start | bytes 442372
  305.2 14.4 %copy-start.22 = (bf16[256,288]{0,1:T(8,128)(2,1)S(1)}, bf16[256,288]{0,1:T(8,128)(2,1)}, u32[]{:S(2)}) copy-start(bf16[256,288]{0,1:T(8,128)(2,1)} %copy-done.21) | copy-start | bytes 442372
  309.0 14.3 %copy-start.24 = (bf16[256,288]{0,1:T(8,128)(2,1)S(1)}, bf16[256,288]{0,1:T(8,128)(2,1)}, u32[]{:S(2)}) copy-start(bf16[256,288]{0,1:T(8,128)(2,1)} %copy-done.23) | copy-start | bytes 442372
  312.8 14.3 %copy-start.26 = (bf16[256,288]{0,1:T(8,128)(2,1)S(1)}, bf16[256,288]{0,1:T(8,128)(2,1)}, u32[]{:S(2)}) copy-start(bf16[256,288]{0,1:T(8,128)(2,1)} %copy-done.25) | copy-start | bytes 442372
  319.7 27.7 %copy-start.29 = (f32[256]{0:T(256)S(1)}, f32[256]{0:T(256)}, u32[]{:S(2)}) copy-start(f32[256]{0:T(256)} %param.19) | copy-start | bytes 3076
  347.4 2.8 copy-start.2
  353.3 146.3 %copy-start.27 = (f32[4608]{0:T(1024)S(1)}, f32[4608]{0:T(1024)}, u32[]{:S(2)}) copy-start(f32[4608]{0:T(1024)} %param.21) | copy-start | bytes 55300
  499.6 3.8 copy-start.3
  506.0 1.7 copy-start.1
Sparse Core Ops, SparseCore 0:
  14.1 129.1 all-reduce.3
  159.9 17.6 all-reduce.5
  353.4 146.1 all-reduce.7
